TPU v7x, 256 devices: a whole 4x4x8 slice. The times are simulated.
256 devices in a mesh: req: 32 (over z, y), mdl: 8 (over x, core).
Axes of the slice: x: 4, y: 4, z: 8, core: 2. Of those that a mesh axis runs over, the one named last changes fastest.
Arguments:
- stream: bfloat16 [24576, 1792], P('req'), may hold values from -6 to 6
- attention_projection_weight: bfloat16 [3, 1792, 1792], P(None, 'mdl'), may hold values from -0.125 to 0.125
- head_output_weight: bfloat16 [1792, 1792], P('mdl'), may hold values from -0.125 to 0.125
- adapter_down_maps: bfloat16 [64, 1792, 16], P('mdl'), may hold values from -0.125 to 0.125
- adapter_up_maps: bfloat16 [2, 1792, 1024], P(None, 'mdl'), may hold values from -1.5 to 1.5
- tenant_adapter_scale: float32 [4], replicated, may hold values from 0.5 to 2
- feedforward_norm_gain: bfloat16 [1792], replicated, may hold values from 0.099609375 to 1.8984375
- feedforward_weight: bfloat16 [3, 1792, 4864], P(None, 'req', 'mdl'), may hold values from -0.125 to 0.125
- prefix_cache_store: bfloat16 [1024, 2, 1792, 128], P('req', None, 'mdl'), may hold values from -140 to 140
- token_adapter_index: int32 [24576], P('req'), may hold values from 0 to 63
- request_token_lengths: int32 [32, 24], P('req'), may hold values from 1 to 192, 768 in all within a row
- request_tenant_index: int32 [768], P('req'), may hold values from 0 to 3
- last_page_holder: int32 [768, 1], replicated, may hold values from 0 to 31; in each aligned block of 24 rows (0 to 23, 24 to 47, ...) at most 2 rows name the same one
- holder_page_slot: int32 [768], replicated, may hold values from 0 to 31
- page_filled_rows: int32 [768], replicated, may hold values from 64 to 128
Outputs:
- layer_out: bfloat16 [24576, 1792], P(('req', 'mdl'))
Inputs may be any that keep to these rules, and one draw needn't show every extreme that they name: `last_page_holder`: within the rows of one index of req (aligned blocks of 24 rows) no holder is named more than 2 times, and one holder exactly 2 times in some blocks. `request_token_lengths`: each row sums to 768; its longest request has exactly 192 tokens.
All inputs are finite; a program needn't handle non-finite values.
Results may differ from a plain program's by a relative error of at most 0.025.
Values may be sent and summed in bfloat16 or wider, within the bound.
A program may use at most 128 MiB of HBM per device.

v0:
```python
import math
import jax
import jax.numpy as jnp
from jax import lax
from jax.sharding import PartitionSpec as P

HEAD_SIZE = 112
WINDOW = 64


def per_device(
    stream,
    attention_projection_weight,
    head_output_weight,
    adapter_down_maps,
    adapter_up_maps,
    tenant_adapter_scale,
    feedforward_norm_gain,
    feedforward_weight,
    prefix_cache_store,
    token_adapter_index,
    request_token_lengths,
    request_tenant_index,
    last_page_holder,
    holder_page_slot,
    page_filled_rows,
):
    tok_count, model_width = stream.shape
    head_column_set = attention_projection_weight.shape[1]
    head_local = head_column_set // HEAD_SIZE
    req_per_dev = request_token_lengths.shape[1]
    rank_total_width = adapter_down_maps.shape[2]
    adapter_number = adapter_up_maps.shape[2] // rank_total_width
    req_devices = lax.axis_size("req")
    req_index = lax.axis_index("req")
    mdl_index = lax.axis_index("mdl")
    row_share = tok_count // lax.axis_size("mdl")
    cap_slots = max(2, (req_per_dev + req_devices - 1) // req_devices + 1)
    projected_rows = jnp.einsum(
        "td,kcd->ktc", stream, attention_projection_weight, preferred_element_type=jnp.float32
    )
    all_onehot = (
        token_adapter_index[:, None] == jnp.arange(adapter_number, dtype=jnp.int32)[None, :]
    )
    holder_count = adapter_down_maps.shape[0]
    holder_rank_rows = jnp.einsum(
        "qf,kfn->qkn", stream, adapter_down_maps, preferred_element_type=jnp.float32
    )
    held_onehot = (
        token_adapter_index[:, None]
        == (mdl_index * holder_count + jnp.arange(holder_count, dtype=jnp.int32))[None, :]
    )
    rank_part = jnp.sum(holder_rank_rows * held_onehot.astype(jnp.float32)[:, :, None], axis=1)
    rank_feat = lax.psum(rank_part.astype(jnp.bfloat16), "mdl")
    broadcast_result = (
        all_onehot.astype(jnp.bfloat16)[:, :, None] * rank_feat[:, None, :]
    ).reshape(tok_count, adapter_number * rank_total_width)
    adapter_column_set = jnp.einsum(
        "iu,pdu->ipd", broadcast_result, adapter_up_maps, preferred_element_type=jnp.float32
    )
    positions = jnp.arange(tok_count, dtype=jnp.int32)
    lengths_row = request_token_lengths[0]
    starts = jnp.cumsum(lengths_row) - lengths_row
    member = (positions[:, None] >= starts[None, :]) & (
        positions[:, None] < (starts + lengths_row)[None, :]
    )
    member_int = member.astype(jnp.int32)
    request_of = jnp.sum(member_int * jnp.arange(req_per_dev, dtype=jnp.int32)[None, :], axis=1)
    relative = positions - jnp.sum(member_int * starts[None, :], axis=1)
    tenant_hot = (
        request_tenant_index[:, None]
        == jnp.arange(tenant_adapter_scale.shape[0], dtype=jnp.int32)[None, :]
    ).astype(jnp.float32)
    request_scale = jnp.sum(tenant_hot * tenant_adapter_scale[None, :], axis=1)
    per_token_scale = jnp.sum(member.astype(jnp.float32) * request_scale[None, :], axis=1)[:, None]
    query_rows = (projected_rows[0] + per_token_scale * adapter_column_set[:, 0]).astype(
        jnp.bfloat16
    )
    key_rows = projected_rows[1].astype(jnp.bfloat16)
    value_row_block = (projected_rows[2] + per_token_scale * adapter_column_set[:, 1]).astype(
        jnp.bfloat16
    )
    owner_column = last_page_holder[:, 0]
    owner_table = owner_column.reshape(req_devices, req_per_dev)
    slot_table = holder_page_slot.reshape(req_devices, req_per_dev)
    owned = (owner_table == req_index).astype(jnp.int32)
    owned_rank = jnp.cumsum(owned, axis=1) - 1
    picked = owned[:, None, :] * (
        owned_rank[:, None, :] == jnp.arange(cap_slots, dtype=jnp.int32)[None, :, None]
    ).astype(jnp.int32)
    send_slot = jnp.sum(picked * slot_table[:, None, :], axis=2)
    fill_table = page_filled_rows.reshape(req_devices, req_per_dev)
    send_fill = jnp.sum(picked * fill_table[:, None, :], axis=2)
    my_owner = lax.dynamic_slice_in_dim(owner_column, req_index * req_per_dev, req_per_dev, 0)
    order_ids = jnp.arange(req_per_dev, dtype=jnp.int32)
    earlier = (my_owner[:, None] == my_owner[None, :]) & (order_ids[:, None] > order_ids[None, :])
    flat_pick = my_owner * cap_slots + jnp.sum(earlier.astype(jnp.int32), axis=1)
    page_inner = prefix_cache_store.shape[1:3]

    def cut_window(slot, fill):
        return lax.dynamic_slice(
            prefix_cache_store, (slot, 0, 0, fill - WINDOW), (1,) + page_inner + (WINDOW,)
        )[0]

    source_pages = jax.vmap(cut_window)(send_slot.reshape(-1), send_fill.reshape(-1))
    source_pages = source_pages.reshape((req_devices, cap_slots) + page_inner + (WINDOW,))
    arrived = lax.all_to_all(source_pages, "req", split_axis=0, concat_axis=0, tiled=True)
    full_mlp = lax.all_gather(feedforward_weight, "req", axis=1, tiled=True)
    full_mlp, arrived = lax.optimization_barrier((full_mlp, arrived))
    chosen = jnp.take(
        arrived.reshape((req_devices * cap_slots,) + page_inner + (WINDOW,)),
        flat_pick,
        axis=0,
        mode="clip",
    )
    prefix = jnp.transpose(chosen, (0, 3, 1, 2))
    key_all = jnp.concatenate(
        [key_rows, prefix[:, :, 0].reshape(req_per_dev * WINDOW, head_column_set)], axis=0
    )
    value_all = jnp.concatenate(
        [value_row_block, prefix[:, :, 1].reshape(req_per_dev * WINDOW, head_column_set)], axis=0
    )
    distance = positions[:, None] - positions[None, :]
    local_ok = (request_of[:, None] == request_of[None, :]) & (distance >= 0) & (distance <= WINDOW)
    key_request = jnp.repeat(jnp.arange(req_per_dev, dtype=jnp.int32), WINDOW)
    key_offset = jnp.tile(jnp.arange(WINDOW, dtype=jnp.int32), req_per_dev)
    prefix_ok = (request_of[:, None] == key_request[None, :]) & (
        key_offset[None, :] >= relative[:, None]
    )
    allowed = jnp.concatenate([local_ok, prefix_ok], axis=1)
    query_heads = query_rows.reshape(tok_count, head_local, HEAD_SIZE)
    key_heads = key_all.reshape(-1, head_local, HEAD_SIZE)
    value_heads = value_all.reshape(-1, head_local, HEAD_SIZE)
    scores = jnp.einsum(
        "thd,shd->hts", query_heads, key_heads, preferred_element_type=jnp.float32
    ) * (1.0 / math.sqrt(HEAD_SIZE))
    masked = jnp.where(allowed[None], scores, -1e30)
    row_max = jnp.max(masked, axis=-1, keepdims=True)
    exp_scores = jnp.exp(masked - row_max)
    weights = (exp_scores / jnp.sum(exp_scores, axis=-1, keepdims=True)).astype(jnp.bfloat16)
    mixed = (
        jnp.einsum("hts,shd->thd", weights, value_heads, preferred_element_type=jnp.float32)
        .astype(jnp.bfloat16)
        .reshape(tok_count, head_column_set)
    )
    attn_part = (
        jnp.dot(mixed, head_output_weight, preferred_element_type=jnp.float32)
        .astype(jnp.bfloat16)
        .astype(jnp.float32)
    )
    gain_wide = feedforward_norm_gain.astype(jnp.float32)[None, :]
    attn_full = lax.psum(attn_part.astype(jnp.bfloat16), "mdl").astype(jnp.float32)
    resid_full = (stream.astype(jnp.float32) + attn_full).astype(jnp.bfloat16)
    resid_wide = resid_full.astype(jnp.float32)
    mean_sq = jnp.mean(resid_wide * resid_wide, axis=1, keepdims=True)
    normed = (resid_wide * lax.rsqrt(mean_sq + 1e-06) * gain_wide).astype(jnp.bfloat16)
    resid_mine = lax.dynamic_slice_in_dim(resid_full, mdl_index * row_share, row_share, 0)
    gate_part = jnp.dot(normed, full_mlp[0], preferred_element_type=jnp.float32)
    up_part = jnp.dot(normed, full_mlp[1], preferred_element_type=jnp.float32)
    hidden = (jax.nn.silu(gate_part) * up_part).astype(jnp.bfloat16)
    mlp_part = (
        jnp.einsum("tf,df->td", hidden, full_mlp[2], preferred_element_type=jnp.float32)
        .astype(jnp.bfloat16)
        .astype(jnp.float32)
    )
    mlp_mine = lax.psum_scatter(
        mlp_part.astype(jnp.bfloat16), "mdl", scatter_dimension=0, tiled=True
    ).astype(jnp.float32)
    return (resid_mine.astype(jnp.float32) + mlp_mine).astype(jnp.bfloat16)


def solution(mesh):
    return jax.shard_map(
        per_device,
        mesh=mesh,
        in_specs=(
            P("req", None),
            P(None, "mdl", None),
            P("mdl", None),
            P("mdl", None, None),
            P(None, "mdl", None),
            P(),
            P(),
            P(None, "req", "mdl"),
            P("req", None, "mdl", None),
            P("req"),
            P("req", None),
            P("req"),
            P(),
            P(),
            P(),
        ),
        out_specs=P(("req", "mdl"), None),
        check_vma=False,
    )
```

profile of v0, /device:TPU:8, one launch (start us, length us, event | category | flops | bytes accessed | tf_op | source)
XLA Modules:
  0.0 343.1 jit_solution(13836156589425205847)
XLA Ops:
  6.5 0.7 all-gather.2.cloned.1.call-update
  7.3 0.7 fusion.46
  8.0 0.1 reshape.216
  8.1 0.1 copy.27
  8.1 0.2 reduce_window_sum.18
  8.3 0.1 copy.26
  8.4 0.8 mul.159
  9.2 0.1 copy.28
  9.2 0.8 mul.162
  10.0 0.1 copy.30
  10.1 0.1 copy.31
  10.2 0.1 sub.51
  10.3 0.1 copy.29
  10.4 0.1 reshape.213
  10.5 0.1 copy.32
  10.6 0.1 add.111
  10.7 11.2 %copy.33 = bf16[32,2,224,128]{2,1,0,3:T(2,128)(2,1)} copy(bf16[32,2,224,128]{3,2,1,0:T(8,128)(2,1)} %param.23) | data formatting | bytes 7340032 | tf_op args[8]
  21.9 14.3 %gather_fusion = bf16[64,2,224,64]{2,1,3,0:T(2,128)(2,1)} fusion(bf16[32,2,224,128]{2,1,0,3:T(2,128)(2,1)} %copy.33, s32[64]{0:T(128)S(1)} %fusion.53), kind=kCustom, calls=%fused_computation | custom fusion | bytes 7341056 | tf_op jit(solution)/shard_map/vmap()/gather | solution.py:101
  36.2 12.9 %all-to-all-start = ((bf16[32,2,2,224,64]{3,2,4,1,0:T(2,128)(2,1)}), bf16[32,2,2,224,64]{3,2,4,1,0:T(2,128)(2,1)}, u32[]{:S(2)}, u32[]{:S(2)}) async-start(bf16[32,2,2,224,64]{3,2,4,1,0:T(2,128)(2,1)} %bitcast.72), calls=%async_computation | async-start | bytes 8388608 | tf_op jit(solution)/shard_map/all_to_all | solution.py:107
  49.2 0.0 all-reduce.2.cloned.1.call-start
  49.2 0.1 copy.24
  49.4 0.1 reduce
  49.5 0.1 ge.45
  49.6 0.1 eq.140
  49.6 3.9 %fusion.23 = f32[3,768,224]{1,2,0:T(8,128)S(1)} fusion(bf16[3,224,1792]{2,1,0:T(8,128)(2,1)S(1)} %copy-done, bf16[768,1792]{1,0:T(8,128)(2,1)} %param.15), kind=kOutput, calls=%fused_computation.37 | convolution fusion | flops 1849688064 | bytes 7225344 | tf_op jit(solution)/shard_map/td,kcd->ktc/dot_general | solution.py:39
  53.6 1.4 copy-done.3
  55.0 0.1 compare_convert_fusion
  55.1 2.8 fusion.67
  58.0 26.8 %psum.14 = bf16[768,16]{0,1:T(8,128)(2,1)S(1)} all-reduce(bf16[768,16]{0,1:T(8,128)(2,1)S(1)} %multiply_reduce_fusion), channel_id=1, replica_groups=mesh['req'=32,'mdl'=8] {'mdl'}, use_global_device_ids=true, to_apply=%region_4.5 | all-reduce | flops 12288 | bytes 49152 | tf_op jit(solution)/shard_map/psum | solution.py:54
  84.7 0.8 fusion.54
  85.5 0.2 convert_reduce_fusion
  85.7 0.8 fusion.52
  86.4 0.1 select_reduce_fusion.3
  86.5 0.1 select_reduce_fusion.2
  86.6 0.1 select_reduce_fusion.1
  86.8 0.1 broadcast_multiply_fusion
  86.9 1.4 fusion.63
  88.3 0.9 fusion.68
  89.2 0.1 fusion.65
  89.3 0.3 fusion.14
  89.6 1.1 add_convert_fusion.3
  90.7 1.3 compare_and_fusion
  91.9 1.4 pad_add_fusion
  93.3 81.0 %all-to-all-done = bf16[32,2,2,224,64]{3,2,4,1,0:T(2,128)(2,1)} async-done(((bf16[32,2,2,224,64]{3,2,4,1,0:T(2,128)(2,1)}), bf16[32,2,2,224,64]{3,2,4,1,0:T(2,128)(2,1)}, u32[]{:S(2)}, u32[]{:S(2)}) %all-to-all-start) | async-done | bytes 3670048 | tf_op jit(solution)/shard_map/all_to_all | solution.py:107
  174.3 5.1 %copy.34 = bf16[32,2,2,224,64]{3,4,2,1,0:T(8,128)(2,1)} copy(bf16[32,2,2,224,64]{3,2,4,1,0:T(2,128)(2,1)} %all-to-all-done) | data formatting | bytes 7340032 | tf_op jit(solution)/shard_map/optimization_barrier | solution.py:109
  179.4 2.8 gather_fusion.1
  182.3 0.2 fusion.64
  182.5 0.4 concatenate.23
  182.9 0.6 copy.35
  183.5 0.4 concatenate.26
  183.9 0.6 copy.36
  184.5 9.5 %fusion.66 = (f32[2,768]{1,0:T(2,128)S(1)}, f32[2,768,2304]{2,1,0:T(8,128)}) fusion(pred[768,2304]{1,0:T(8,128)(4,1)} %pad_add_fusion, bf16[768,2,112]{0,2,1:T(8,128)(2,1)S(1)} %copy-done.7, bf16[1536,2,112]{0,2,1:T(8,128)(2,1)S(1)} %copy.36, bf16[768,2,112]{0,2,1:T(8,128)(2,1)S(1)} %bitcast.82), kind=kOutput, calls=%fused_computation.102 | convolution fusion | flops 808945920 | bytes 17307648 | tf_op jit(solution)/shard_map/sub | solution.py:139
  194.1 7.6 %fusion.32 = bf16[2,112,768]{2,1,0:T(8,128)(2,1)S(1)} fusion(f32[2,768,2304]{2,1,0:T(8,128)} %get-tuple-element.26, f32[2,768]{1,0:T(2,128)S(1)} %get-tuple-element.25, bf16[1536,2,112]{0,2,1:T(8,128)(2,1)S(1)} %copy.35, bf16[768,2,112]{0,2,1:T(8,128)(2,1)S(1)} %copy-done.6), kind=kOutput, calls=%fused_computation.39 | convolution fusion | flops 802037760 | bytes 15538176 | tf_op jit(solution)/shard_map/hts,shd->thd/dot_general | solution.py:142
  201.7 2.5 convolution_convert_fusion
  204.2 0.0 all-reduce.2.cloned.1.call-update
  204.2 0.3 reduce-scatter.2.cloned.1.call-start
  204.5 72.0 %all-reduce.2.cloned.1.call-done = bf16[768,1792]{1,0:T(8,128)(2,1)} async-done(((bf16[768,1792]{1,0:T(8,128)(2,1)}), bf16[768,1792]{1,0:T(8,128)(2,1)}) %all-reduce.2.cloned.1.call-update) | async-done | bytes 2752528 | tf_op jit(solution)/shard_map/psum | solution.py:152
  276.4 3.7 %fusion.6 = (f32[768]{0:T(1024)S(1)}, bf16[768,1792]{1,0:T(8,128)(2,1)S(1)}) fusion(bf16[768,1792]{1,0:T(8,128)(2,1)} %all-reduce.2.cloned.1.call-done, bf16[768,1792]{1,0:T(8,128)(2,1)} %param.15), kind=kLoop, calls=%fused_computation.14 | loop fusion | flops 9633024 | bytes 8260608 | tf_op jit(solution)/shard_map/reduce_sum | solution.py:155
  280.1 1.5 copy-done.2
  281.7 5.1 %fusion.18 = f32[768,608]{0,1:T(8,128)} fusion(bf16[3,1792,608]{2,1,0:T(8,128)(2,1)} %all-gather.2.cloned.1.call-done, bf16[768,1792]{1,0:T(8,128)(2,1)S(1)} %get-tuple-element.14, f32[1792]{0:T(1024)S(1)} %convert_element_type.118, f32[768]{0:T(1024)S(1)} %add_rsqrt_fusion), kind=kOutput, calls=%fused_computation.31 | convolution fusion | flops 1679032320 | bytes 6924288 | tf_op jit(solution)/shard_map/dot_general | solution.py:158
  286.7 10.6 %convolution_convert_fusion.1 = bf16[768,1792]{1,0:T(8,128)(2,1)} fusion(bf16[3,1792,608]{2,1,0:T(8,128)(2,1)} %all-gather.2.cloned.1.call-done, f32[768,608]{0,1:T(8,128)} %fusion.18, bf16[768,1792]{1,0:T(8,128)(2,1)} %copy-done.2, f32[1792]{0:T(1024)S(1)} %convert_element_type.118, f32[768]{0:T(1024)S(1)} %add_rsqrt_fusion), kind=kOutput, calls=%fused_computation.20 | convolution fusion | flops 3356737536 | bytes 11970560 | tf_op jit(solution)/shard_map/tf,df->td/dot_general | solution.py:162
  297.3 0.0 reduce-scatter.2.cloned.1.call-update
  297.4 37.3 %reduce-scatter.2.cloned.1.call-done = bf16[96,1792]{1,0:T(8,128)(2,1)} async-done(((bf16[768,1792]{1,0:T(8,128)(2,1)}), bf16[96,1792]{1,0:T(8,128)(2,1)}) %reduce-scatter.2.cloned.1.call-update) | async-done | bytes 344080 | tf_op jit(solution)/shard_map/reduce_scatter | solution.py:166
  334.7 1.9 add_convert_fusion.1
  (44 shorter events, 0.3 us)
Async XLA Ops:
  6.5 43.1 %copy-start = (bf16[3,224,1792]{2,1,0:T(8,128)(2,1)S(1)}, bf16[3,224,1792]{2,1,0:T(8,128)(2,1)}, u32[]{:S(2)}) copy-start(bf16[3,224,1792]{2,1,0:T(8,128)(2,1)} %param.16) | copy-start | bytes 7225348
  6.5 167.8 %all-gather.2.cloned.1.call-start = ((), (), s32[]{:S(2)}) async-start(), calls=%async_computation.2 | async-start | bytes 7096320 | tf_op jit(solution)/shard_map/all_gather | solution.py:108
  36.2 13.0 %copy-start.10 = (s32[1,24]{1,0:T(1,128)S(1)}, s32[1,24]{1,0:T(1,128)}, u32[]{:S(2)}) copy-start(s32[1,24]{1,0:T(1,128)} %param.25) | copy-start | bytes 292
  36.2 138.1 %all-to-all-start = ((bf16[32,2,2,224,64]{3,2,4,1,0:T(2,128)(2,1)}), bf16[32,2,2,224,64]{3,2,4,1,0:T(2,128)(2,1)}, u32[]{:S(2)}, u32[]{:S(2)}) async-start(bf16[32,2,2,224,64]{3,2,4,1,0:T(2,128)(2,1)} %bitcast.72), calls=%async_computation | async-start | bytes 8388608 | tf_op jit(solution)/shard_map/all_to_all | solution.py:107
  49.2 227.3 %all-reduce.2.cloned.1.call-start = ((), (), s32[]{:S(2)}) async-start(), calls=%async_computation.3 | async-start | bytes 5505024 | tf_op jit(solution)/shard_map/psum | solution.py:152
  49.6 5.4 %copy-start.8 = (s32[768]{0:T(1024)S(1)}, s32[768]{0:T(1024)}, u32[]{:S(2)}) copy-start(s32[768]{0:T(1024)} %param.24) | copy-start | bytes 9220
  49.6 5.4 %copy-start.5 = (bf16[8,1792,16]{1,2,0:T(8,128)(2,1)S(1)}, bf16[8,1792,16]{1,2,0:T(8,128)(2,1)}, u32[]{:S(2)}) copy-start(bf16[8,1792,16]{1,2,0:T(8,128)(2,1)} %param.18) | copy-start | bytes 1376260
  53.6 1.4 copy-start.3
  55.0 31.5 %copy-start.12 = (f32[4]{0:T(128)S(1)}, f32[4]{0:T(128)}, u32[]{:S(2)}) copy-start(f32[4]{0:T(128)} %param.20) | copy-start | bytes 52
  55.0 31.4 %copy-start.13 = (s32[24]{0:T(128)S(1)}, s32[24]{0:T(128)}, u32[]{:S(2)}) copy-start(s32[24]{0:T(128)} %param.26) | copy-start | bytes 292
  57.9 30.4 %copy-start.11 = (bf16[2,224,1024]{2,1,0:T(8,128)(2,1)S(1)}, bf16[2,224,1024]{2,1,0:T(8,128)(2,1)}, u32[]{:S(2)}) copy-start(bf16[2,224,1024]{2,1,0:T(8,128)(2,1)} %param.19) | copy-start | bytes 2752516
  182.9 1.6 copy-start.7
  184.5 9.6 %copy-start.6 = (bf16[768,2,112]{0,2,1:T(8,128)(2,1)S(1)}, bf16[768,2,112]{0,2,1:T(8,128)(2,1)}, u32[]{:S(2)}) copy-start(bf16[768,2,112]{0,2,1:T(8,128)(2,1)} %get-tuple-element.21) | copy-start | bytes 1032196
  194.1 7.6 %copy-start.4 = (bf16[224,1792]{1,0:T(8,128)(2,1)S(1)}, bf16[224,1792]{1,0:T(8,128)(2,1)}, u32[]{:S(2)}) copy-start(bf16[224,1792]{1,0:T(8,128)(2,1)} %param.17) | copy-start | bytes 2408452
  201.6 2.8 copy-start.9
  204.2 130.5 %reduce-scatter.2.cloned.1.call-start = ((), (), s32[]{:S(2)}) async-start(), calls=%async_computation.4 | async-start | bytes 3096576 | tf_op jit(solution)/shard_map/reduce_scatter | solution.py:166
  280.1 1.6 copy-start.2
  286.7 49.9 %copy-start.1 = (bf16[3,224,1792]{2,1,0:T(8,128)(2,1)S(1)}, bf16[3,224,1792]{2,1,0:T(8,128)(2,1)}, u32[]{:S(2)}) copy-start(bf16[3,224,1792]{2,1,0:T(8,128)(2,1)} %param.16) | copy-start | bytes 7225348
Sparse Core Ops, SparseCore 0:
  10.0 159.9 all-gather.1
  204.3 72.0 all-reduce.1
  297.5 37.1 reduce-scatter.1
where the time goes:
time: 344 us; the launch traced here: 343 us
  waiting for transfers between devices  191 us (56%)
  local copies, waits for them, and re-layouts  43.6 us (13%)
  matrix products  42.9 us (12%)
  blocking collectives  26.8 us (8%)
  between operations  13.5 us (4%)
  starting transfers between devices  13.2 us (4%)
  other arithmetic  12.1 us (4%)
    all_to_all x1, waiting for transfers between devices, per_device(): lax.all_to_all(source_pages, 'req', split_axis=0, concat_axis=0, tiled=True)  81 us
    psum x1, waiting for transfers between devices, per_device(): lax.psum(attn_part.astype(jnp.bfloat16), 'mdl').astype(jnp.float32)  72 us
    reduce_scatter x1, waiting for transfers between devices, per_device(): lax.psum_scatter(mlp_part.astype(jnp.bfloat16), 'mdl', scatter_dimension=...  37.3 us
    psum x1, blocking collectives, per_device(): rank_feat = lax.psum(rank_part.astype(jnp.bfloat16), 'mdl')  26.8 us
    gather x1, local copies, waits for them, and re-layouts, cut_window(): lax.dynamic_slice(prefix_cache_store, (slot, 0, 0, fill - WINDOW), (1,) +...  14.3 us
    unnamed x29, local copies, waits for them, and re-layouts  14.2 us
    all_to_all x1, starting transfers between devices, per_device(): lax.all_to_all(source_pages, 'req', split_axis=0, concat_axis=0, tiled=True)  12.9 us
    dot_general x1, matrix products, per_device(): jnp.einsum('tf,df->td', hidden, full_mlp[2], preferred_element_type=jnp.f...  10.6 us
  transfers between devices with their start and end apart: 4, of which 3 were waited for; matrix products, arithmetic and copies ran while one was open for 13% of the time, Pallas kernels for 0%

commit v1 on v0

--- a/solution.py
+++ b/solution.py
@@ -6,6 +6,7 @@
 
 HEAD_SIZE = 112
 WINDOW = 64
+supply_regions = lambda point, mesh_ax: jnp.sum(lax.all_gather(point, mesh_ax), 0)
 
 
 def per_device(
@@ -51,7 +52,7 @@
         == (mdl_index * holder_count + jnp.arange(holder_count, dtype=jnp.int32))[None, :]
     )
     rank_part = jnp.sum(holder_rank_rows * held_onehot.astype(jnp.float32)[:, :, None], axis=1)
-    rank_feat = lax.psum(rank_part.astype(jnp.bfloat16), "mdl")
+    rank_feat = supply_regions(rank_part.astype(jnp.bfloat16), "mdl")
     broadcast_result = (
         all_onehot.astype(jnp.bfloat16)[:, :, None] * rank_feat[:, None, :]
     ).reshape(tok_count, adapter_number * rank_total_width)

time: 344 us -> 344 us (level)
  waiting for transfers between devices: 191 us -> 205 us
  blocking collectives: 26.8 us -> 13.4 us
    psum x1 -> x0, blocking collectives: 26.8 us -> none  [per_device(): rank_feat = lax.psum(rank_part.astype(jnp.bfloat16), 'mdl')]
    all_to_all x1, waiting for transfers between devices: 81 us -> 94.7 us  [per_device(): lax.all_to_all(source_pages, 'req', split_axis=0, concat_axis=0, tiled=True)]
    all_gather x0 -> x1, blocking collectives: none -> 13.4 us  [lax.all_gather(point, mesh_ax)]
    unnamed x29 -> x30, local copies, waits for them, and re-layouts: 14.2 us -> 14.2 us
where the time goes in v1:
time: 344 us; the launch traced here: 343 us
  waiting for transfers between devices  205 us (60%)
  local copies, waits for them, and re-layouts  43.6 us (13%)
  matrix products  42.4 us (12%)
  between operations  13.5 us (4%)
  blocking collectives  13.4 us (4%)
  starting transfers between devices  13.2 us (4%)
  other arithmetic  12.3 us (4%)
    all_to_all x1, waiting for transfers between devices, per_device(): lax.all_to_all(source_pages, 'req', split_axis=0, concat_axis=0, tiled=True)  94.7 us
    psum x1, waiting for transfers between devices, per_device(): lax.psum(attn_part.astype(jnp.bfloat16), 'mdl').astype(jnp.float32)  72.2 us
    reduce_scatter x1, waiting for transfers between devices, per_device(): lax.psum_scatter(mlp_part.astype(jnp.bfloat16), 'mdl', scatter_dimension=...  37.4 us
    gather x1, local copies, waits for them, and re-layouts, cut_window(): lax.dynamic_slice(prefix_cache_store, (slot, 0, 0, fill - WINDOW), (1,) +...  14.3 us
    unnamed x30, local copies, waits for them, and re-layouts  14.2 us
    all_gather x1, blocking collectives, lax.all_gather(point, mesh_ax)  13.4 us
    all_to_all x1, starting transfers between devices, per_device(): lax.all_to_all(source_pages, 'req', split_axis=0, concat_axis=0, tiled=True)  12.9 us
    dot_general x1, matrix products, per_device(): jnp.einsum('tf,df->td', hidden, full_mlp[2], preferred_element_type=jnp.f...  10.6 us
  transfers between devices with their start and end apart: 4, of which 3 were waited for; matrix products, arithmetic and copies ran while one was open for 13% of the time, Pallas kernels for 0%

profile of v1, /device:TPU:8, one launch (start us, length us, event | category | flops | bytes accessed | tf_op | source)
XLA Modules:
  0.0 343.4 jit_solution(14834773080529675949)
XLA Ops:
  6.5 0.7 all-gather.3.cloned.1.call-update
  7.3 0.7 fusion.46
  8.0 0.1 reshape.224
  8.1 0.1 copy.33
  8.1 0.2 reduce_window_sum.18
  8.3 0.1 copy.32
  8.4 0.8 mul.159
  9.2 0.1 copy.34
  9.2 0.8 mul.162
  10.0 0.1 copy.36
  10.1 0.1 copy.37
  10.2 0.1 sub.51
  10.3 0.1 copy.35
  10.4 0.1 reshape.221
  10.5 0.1 copy.38
  10.6 0.1 add.109
  10.7 11.2 %copy.39 = bf16[32,2,224,128]{2,1,0,3:T(2,128)(2,1)} copy(bf16[32,2,224,128]{3,2,1,0:T(8,128)(2,1)} %param.23) | data formatting | bytes 7340032 | tf_op args[8]
  21.9 14.3 %gather_fusion = bf16[64,2,224,64]{2,1,3,0:T(2,128)(2,1)} fusion(bf16[32,2,224,128]{2,1,0,3:T(2,128)(2,1)} %copy.39, s32[64]{0:T(128)S(1)} %fusion.53), kind=kCustom, calls=%fused_computation | custom fusion | bytes 7341056 | tf_op jit(solution)/shard_map/vmap()/gather | solution.py:102
  36.3 12.9 %all-to-all-start = ((bf16[32,2,2,224,64]{3,2,4,1,0:T(2,128)(2,1)}), bf16[32,2,2,224,64]{3,2,4,1,0:T(2,128)(2,1)}, u32[]{:S(2)}, u32[]{:S(2)}) async-start(bf16[32,2,2,224,64]{3,2,4,1,0:T(2,128)(2,1)} %bitcast.77), calls=%async_computation | async-start | bytes 8388608 | tf_op jit(solution)/shard_map/all_to_all | solution.py:108
  49.2 0.0 all-reduce.2.cloned.1.call-start
  49.2 0.1 copy.30
  49.4 0.1 reduce.1
  49.5 0.1 ge.45
  49.6 0.1 eq.140
  49.7 0.1 compare_convert_fusion
  49.7 3.0 fusion.67
  52.7 13.4 %all-gather = bf16[6144,16]{0,1:T(8,128)(2,1)S(1)} all-gather(bf16[768,16]{0,1:T(8,128)(2,1)S(1)} %multiply_reduce_fusion), channel_id=2, replica_groups=mesh['req'=32,'mdl'=8] {'mdl'}, dimensions={0}, use_global_device_ids=true | all-gather | bytes 221184 | tf_op jit(solution)/shard_map/all_gather | solution.py:9
  66.2 2.1 fusion.23
  68.2 1.4 copy-done.4
  69.7 0.8 fusion.54
  70.4 0.2 convert_reduce_fusion
  70.6 0.8 fusion.52
  71.4 0.1 select_reduce_fusion.3
  71.5 0.1 select_reduce_fusion.2
  71.6 0.1 select_reduce_fusion.1
  71.7 0.1 bitcast_reduce_fusion
  71.9 0.1 broadcast_multiply_fusion
  72.0 1.4 fusion.63
  73.4 2.1 fusion.68
  75.5 0.1 fusion.65
  75.6 0.3 fusion.14
  75.9 1.1 add_convert_fusion.3
  77.0 1.3 compare_and_fusion
  78.2 1.4 pad_add_fusion
  79.6 94.7 %all-to-all-done = bf16[32,2,2,224,64]{3,2,4,1,0:T(2,128)(2,1)} async-done(((bf16[32,2,2,224,64]{3,2,4,1,0:T(2,128)(2,1)}), bf16[32,2,2,224,64]{3,2,4,1,0:T(2,128)(2,1)}, u32[]{:S(2)}, u32[]{:S(2)}) %all-to-all-start) | async-done | bytes 3670048 | tf_op jit(solution)/shard_map/all_to_all | solution.py:108
  174.4 5.1 %copy.40 = bf16[32,2,2,224,64]{3,4,2,1,0:T(8,128)(2,1)} copy(bf16[32,2,2,224,64]{3,2,4,1,0:T(2,128)(2,1)} %all-to-all-done) | data formatting | bytes 7340032 | tf_op jit(solution)/shard_map/optimization_barrier | solution.py:110
  179.5 2.8 gather_fusion.1
  182.3 0.2 fusion.64
  182.5 0.4 concatenate.23
  182.9 0.6 copy.41
  183.5 0.4 concatenate.26
  183.9 0.6 copy.42
  184.5 9.6 %fusion.66 = (f32[2,768]{1,0:T(2,128)S(1)}, f32[2,768,2304]{2,1,0:T(8,128)}) fusion(pred[768,2304]{1,0:T(8,128)(4,1)} %pad_add_fusion, bf16[768,2,112]{0,2,1:T(8,128)(2,1)S(1)} %copy-done.8, bf16[1536,2,112]{0,2,1:T(8,128)(2,1)S(1)} %copy.42, bf16[768,2,112]{0,2,1:T(8,128)(2,1)S(1)} %bitcast.88), kind=kOutput, calls=%fused_computation.103 | convolution fusion | flops 808945920 | bytes 17307648 | tf_op jit(solution)/shard_map/sub | solution.py:140
  194.1 7.6 %fusion.32 = bf16[2,112,768]{2,1,0:T(8,128)(2,1)S(1)} fusion(f32[2,768,2304]{2,1,0:T(8,128)} %get-tuple-element.26, f32[2,768]{1,0:T(2,128)S(1)} %get-tuple-element.25, bf16[1536,2,112]{0,2,1:T(8,128)(2,1)S(1)} %copy.41, bf16[768,2,112]{0,2,1:T(8,128)(2,1)S(1)} %copy-done.7), kind=kOutput, calls=%fused_computation.39 | convolution fusion | flops 802037760 | bytes 15538176 | tf_op jit(solution)/shard_map/hts,shd->thd/dot_general | solution.py:143
  201.7 2.5 convolution_convert_fusion
  204.2 0.0 all-reduce.2.cloned.1.call-update
  204.2 0.3 reduce-scatter.2.cloned.1.call-start
  204.5 72.2 %all-reduce.2.cloned.1.call-done = bf16[768,1792]{1,0:T(8,128)(2,1)} async-done(((bf16[768,1792]{1,0:T(8,128)(2,1)}), bf16[768,1792]{1,0:T(8,128)(2,1)}) %all-reduce.2.cloned.1.call-update) | async-done | bytes 2752528 | tf_op jit(solution)/shard_map/psum | solution.py:153
  276.7 3.7 %fusion.6 = (f32[768]{0:T(1024)S(1)}, bf16[768,1792]{1,0:T(8,128)(2,1)S(1)}) fusion(bf16[768,1792]{1,0:T(8,128)(2,1)} %all-reduce.2.cloned.1.call-done, bf16[768,1792]{1,0:T(8,128)(2,1)} %param.15), kind=kLoop, calls=%fused_computation.14 | loop fusion | flops 9633024 | bytes 8260608 | tf_op jit(solution)/shard_map/reduce_sum | solution.py:156
  280.4 1.5 copy-done.3
  281.9 5.1 %fusion.18 = f32[768,608]{0,1:T(8,128)} fusion(bf16[3,1792,608]{2,1,0:T(8,128)(2,1)} %all-gather.3.cloned.1.call-done, bf16[768,1792]{1,0:T(8,128)(2,1)S(1)} %get-tuple-element.14, f32[1792]{0:T(1024)S(1)} %convert_element_type.131, f32[768]{0:T(1024)S(1)} %add_rsqrt_fusion), kind=kOutput, calls=%fused_computation.31 | convolution fusion | flops 1679032320 | bytes 6924288 | tf_op jit(solution)/shard_map/dot_general | solution.py:159
  287.0 10.6 %convolution_convert_fusion.1 = bf16[768,1792]{1,0:T(8,128)(2,1)} fusion(bf16[3,1792,608]{2,1,0:T(8,128)(2,1)} %all-gather.3.cloned.1.call-done, f32[768,608]{0,1:T(8,128)} %fusion.18, bf16[768,1792]{1,0:T(8,128)(2,1)} %copy-done.3, f32[1792]{0:T(1024)S(1)} %convert_element_type.131, f32[768]{0:T(1024)S(1)} %add_rsqrt_fusion), kind=kOutput, calls=%fused_computation.20 | convolution fusion | flops 3356737536 | bytes 11970560 | tf_op jit(solution)/shard_map/tf,df->td/dot_general | solution.py:163
  297.6 37.4 %reduce-scatter.2.cloned.1.call-done = bf16[96,1792]{1,0:T(8,128)(2,1)} async-done(((bf16[768,1792]{1,0:T(8,128)(2,1)}), bf16[96,1792]{1,0:T(8,128)(2,1)}) %reduce-scatter.2.cloned.1.call-update) | async-done | bytes 344080 | tf_op jit(solution)/shard_map/reduce_scatter | solution.py:167
  335.0 1.9 add_convert_fusion.1
  (46 shorter events, 0.3 us)
Async XLA Ops:
  6.5 59.6 %copy-start = (bf16[3,224,1792]{2,1,0:T(8,128)(2,1)S(1)}, bf16[3,224,1792]{2,1,0:T(8,128)(2,1)}, u32[]{:S(2)}) copy-start(bf16[3,224,1792]{2,1,0:T(8,128)(2,1)} %param.16) | copy-start | bytes 7225348
  6.5 167.8 %all-gather.3.cloned.1.call-start = ((), (), s32[]{:S(2)}) async-start(), calls=%async_computation.2 | async-start | bytes 7096320 | tf_op jit(solution)/shard_map/all_gather | solution.py:109
  36.2 13.0 %copy-start.11 = (s32[1,24]{1,0:T(1,128)S(1)}, s32[1,24]{1,0:T(1,128)}, u32[]{:S(2)}) copy-start(s32[1,24]{1,0:T(1,128)} %param.25) | copy-start | bytes 292
  36.2 13.4 %copy-start.9 = (s32[768]{0:T(1024)S(1)}, s32[768]{0:T(1024)}, u32[]{:S(2)}) copy-start(s32[768]{0:T(1024)} %param.24) | copy-start | bytes 9220
  36.3 13.5 %copy-start.6 = (bf16[8,1792,16]{1,2,0:T(8,128)(2,1)S(1)}, bf16[8,1792,16]{1,2,0:T(8,128)(2,1)}, u32[]{:S(2)}) copy-start(bf16[8,1792,16]{1,2,0:T(8,128)(2,1)} %param.18) | copy-start | bytes 1376260
  36.3 138.1 %all-to-all-start = ((bf16[32,2,2,224,64]{3,2,4,1,0:T(2,128)(2,1)}), bf16[32,2,2,224,64]{3,2,4,1,0:T(2,128)(2,1)}, u32[]{:S(2)}, u32[]{:S(2)}) async-start(bf16[32,2,2,224,64]{3,2,4,1,0:T(2,128)(2,1)} %bitcast.77), calls=%async_computation | async-start | bytes 8388608 | tf_op jit(solution)/shard_map/all_to_all | solution.py:108
  49.2 227.5 %all-reduce.2.cloned.1.call-start = ((), (), s32[]{:S(2)}) async-start(), calls=%async_computation.3 | async-start | bytes 5505024 | tf_op jit(solution)/shard_map/psum | solution.py:153
  49.7 16.4 %copy-start.2 = (bf16[768,1792]{1,0:T(8,128)(2,1)S(1)}, bf16[768,1792]{1,0:T(8,128)(2,1)}, u32[]{:S(2)}) copy-start(bf16[768,1792]{1,0:T(8,128)(2,1)} %param.15) | copy-start | bytes 8257540
  66.1 5.2 %copy-start.12 = (f32[4]{0:T(128)S(1)}, f32[4]{0:T(128)}, u32[]{:S(2)}) copy-start(f32[4]{0:T(128)} %param.20) | copy-start | bytes 52
  66.2 5.2 %copy-start.13 = (s32[24]{0:T(128)S(1)}, s32[24]{0:T(128)}, u32[]{:S(2)}) copy-start(s32[24]{0:T(128)} %param.26) | copy-start | bytes 292
  68.2 1.4 copy-start.4
  182.9 1.6 copy-start.8
  184.5 9.6 %copy-start.7 = (bf16[768,2,112]{0,2,1:T(8,128)(2,1)S(1)}, bf16[768,2,112]{0,2,1:T(8,128)(2,1)}, u32[]{:S(2)}) copy-start(bf16[768,2,112]{0,2,1:T(8,128)(2,1)} %get-tuple-element.21) | copy-start | bytes 1032196
  194.1 7.6 %copy-start.5 = (bf16[224,1792]{1,0:T(8,128)(2,1)S(1)}, bf16[224,1792]{1,0:T(8,128)(2,1)}, u32[]{:S(2)}) copy-start(bf16[224,1792]{1,0:T(8,128)(2,1)} %param.17) | copy-start | bytes 2408452
  201.7 2.8 copy-start.10
  204.2 130.8 %reduce-scatter.2.cloned.1.call-start = ((), (), s32[]{:S(2)}) async-start(), calls=%async_computation.4 | async-start | bytes 3096576 | tf_op jit(solution)/shard_map/reduce_scatter | solution.py:167
  280.3 1.6 copy-start.3
  287.0 49.9 %copy-start.1 = (bf16[3,224,1792]{2,1,0:T(8,128)(2,1)S(1)}, bf16[3,224,1792]{2,1,0:T(8,128)(2,1)}, u32[]{:S(2)}) copy-start(bf16[3,224,1792]{2,1,0:T(8,128)(2,1)} %param.16) | copy-start | bytes 7225348
Sparse Core Ops, SparseCore 0:
  10.0 159.9 all-gather.2
  204.3 72.3 all-reduce.1
  297.7 37.2 reduce-scatter.1
